TPU v7x, 32 devices: a whole 2x2x4 slice. The times are simulated.
32 devices in a mesh: rad: 32 (over z, y, x, core), lat: 1.
Axes of the slice: x: 2, y: 2, z: 4, core: 2. Of those that a mesh axis runs over, the one named last changes fastest.
Arguments:
- nonlinear_samples: bfloat16 [32, 2, 1536, 3072], P('rad', None, 'lat'), may hold values from -6 to 6
- legendre: bfloat16 [256, 1536, 1024], P('rad', 'lat'), may hold values from -0.15625 to 0.15625
- assign: int32 [256], replicated, may hold values from 0 to 255, each once
- counts: int32 [256], replicated, may hold values from 513 to 1024, as said below
- spectral_state: float32 [1024, 256, 128], P('lat', 'rad'), may hold values from -6 to 6
- inverses: float32 [1024, 4, 8, 8], P('lat'), may hold values from -1 to 1
Outputs:
- advanced: float32 [1024, 256, 128], P('lat', 'rad')
Inputs may be any that keep to these rules, and one draw needn't show every extreme that they name: Slot s carries order assign[s]; each order 0 to 255 stands in exactly one slot. counts[m] is at most 1024 - m, and order 0 has 1024 live degrees.
All inputs are finite; a program needn't handle non-finite values.
Results may differ from a plain program's by a relative error of at most 0.0034.
Values may be sent and summed in bfloat16 or wider, within the bound.
No kernel may reach another device: no remote copies, remote signals or barrier semaphores. Data moves between devices by JAX's collectives and lax.ppermute only.
A program may use at most 192 MiB of HBM per device.

v0:
```python
import math

import jax
import jax.numpy as jnp
from jax import lax
from jax.sharding import PartitionSpec as P


def trig_table(assign, lon_count):
    longitude = jnp.arange(lon_count, dtype=jnp.int32)
    phases = longitude[:, None] * assign[None, :] % lon_count
    angles = phases.astype(jnp.float32) * (2.0 * math.pi / lon_count)
    normalizing_multiplier = 1.0 / math.sqrt(lon_count)
    cosine = (jnp.cos(angles) * normalizing_multiplier).astype(jnp.bfloat16)
    sine = (-jnp.sin(angles) * normalizing_multiplier).astype(jnp.bfloat16)
    return jnp.stack([cosine, sine], axis=2).reshape(lon_count, 2 * assign.shape[0])


def radial_step(spectral_state, source, inverses, degree):
    deg_rows, slot_count, width = spectral_state.shape
    shell_number = width // 4
    blk_size = inverses.shape[2]
    blk_count = shell_number // blk_size
    field_now = spectral_state.reshape(deg_rows, slot_count, 4, shell_number)
    zero_rim = jnp.zeros((deg_rows, slot_count, 4, 1), jnp.float32)
    outward = jnp.concatenate([field_now[..., 1:], zero_rim], axis=3)
    inward = jnp.concatenate([zero_rim, field_now[..., :-1]], axis=3)
    radial_spacing = 0.65 / (shell_number + 1)
    radius = 0.35 + 0.65 * (jnp.arange(shell_number, dtype=jnp.float32) + 1.0) / (shell_number + 1)
    ratios = radial_spacing / radius
    degree_term = degree[:, None, None, None] * (degree[:, None, None, None] + 1.0)
    central = 0.5 * radial_spacing * radial_spacing * degree_term / (radius * radius)
    right_side = (
        field_now + 0.5 * (outward - 2.0 * field_now + inward) + 0.5 * ratios * (outward - inward)
    )
    right_side = (
        right_side - central * field_now + source.reshape(deg_rows, slot_count, 4, shell_number)
    )
    lower_link = -0.5 * (1.0 - ratios[0::blk_size])
    upper_link = -0.5 * (1.0 + ratios[blk_size - 1 :: blk_size])
    blocks = jnp.moveaxis(right_side.reshape(deg_rows, slot_count, 4, blk_count, blk_size), 3, 0)
    block_inverse = jnp.moveaxis(inverses, 1, 0)
    first_unit = (jnp.arange(blk_size, dtype=jnp.int32) == 0).astype(jnp.float32)
    start_carry = jnp.zeros((deg_rows, slot_count, 4), jnp.float32)

    def forward(carried, items):
        matrix, block, link = items
        block = block - link * carried[..., None] * first_unit
        result = jnp.einsum("lij,locj->loci", matrix, block, precision=lax.Precision.HIGHEST)
        return (result[..., blk_size - 1], result)

    def inverse_sweep(carried, items):
        matrix, partial_solution, link = items
        result = (
            partial_solution - link * carried[..., None] * matrix[:, None, None, :, blk_size - 1]
        )
        return (result[..., 0], result)

    _, forward_blocks = lax.scan(forward, start_carry, (block_inverse, blocks, lower_link))
    _, solved = lax.scan(
        inverse_sweep, start_carry, (block_inverse, forward_blocks, upper_link), reverse=True
    )
    return jnp.moveaxis(solved, 0, 3).reshape(deg_rows, slot_count, 4 * shell_number)


def body(nonlinear_samples, legendre, assign, counts, spectral_state, inverses):
    rad_local = nonlinear_samples.shape[0]
    lat_local = nonlinear_samples.shape[2]
    lon_count = nonlinear_samples.shape[3]
    order_total = assign.shape[0]
    order_local = legendre.shape[0]
    degree_local = spectral_state.shape[0]
    shell_grand_number = spectral_state.shape[2] // 4
    table = trig_table(assign, lon_count)
    flat_rows = nonlinear_samples.reshape(rad_local * 2 * lat_local, lon_count)
    fourier_modes = jnp.dot(flat_rows, table, preferred_element_type=jnp.float32).astype(
        jnp.bfloat16
    )
    fourier_modes = fourier_modes.reshape(rad_local, 2, lat_local, order_total, 2)
    permuted_dims = lax.all_to_all(fourier_modes, "rad", split_axis=3, concat_axis=0, tiled=True)
    columns = lax.all_to_all(legendre, "lat", split_axis=2, concat_axis=1, tiled=True)
    whole = lax.all_gather(permuted_dims, "lat", axis=2, tiled=True)
    band_total = lax.axis_size("lat")
    legendre_table_bands = columns.reshape(order_local, band_total, lat_local, degree_local)
    value_bands = whole.reshape(shell_grand_number, 2, band_total, lat_local, order_local, 2)
    partial_value = jnp.einsum(
        "obtl,rfbtok->blofkr", legendre_table_bands, value_bands, preferred_element_type=jnp.float32
    )
    partial_value = lax.optimization_barrier(partial_value.astype(jnp.bfloat16)).astype(jnp.float32)
    summed = jnp.sum(partial_value, axis=0).reshape(
        degree_local, order_local, 4 * shell_grand_number
    )
    rad_position = lax.axis_index("rad")
    lat_position = lax.axis_index("lat")
    my_orders = lax.dynamic_slice_in_dim(assign, rad_position * order_local, order_local, 0)
    order_ids = jnp.arange(order_total, dtype=jnp.int32)
    my_counts = jnp.sum(
        jnp.where(my_orders[:, None] == order_ids[None, :], counts[None, :], 0), axis=1
    )
    degree_ids = lat_position * degree_local + jnp.arange(degree_local, dtype=jnp.int32)
    limits = my_orders + my_counts
    live = (degree_ids[:, None] >= my_orders[None, :]) & (degree_ids[:, None] < limits[None, :])
    source = jnp.where(live[:, :, None], summed, jnp.zeros_like(summed))
    return radial_step(spectral_state, source, inverses, degree_ids.astype(jnp.float32))


def solution(mesh):
    return jax.shard_map(
        body,
        mesh=mesh,
        in_specs=(
            P("rad", None, "lat", None),
            P("rad", "lat", None),
            P(),
            P(),
            P("lat", "rad", None),
            P("lat", None, None, None),
        ),
        out_specs=P("lat", "rad", None),
        check_vma=False,
    )
```

profile of v0, /device:TPU:0, one launch (start us, length us, event | category | flops | bytes accessed | tf_op | source)
XLA Modules:
  0.0 1479.2 jit_solution(6106090014343111707)
XLA Ops:
  0.0 14.1 multiply_convert_fusion.1
  14.4 5.8 copy.54
  20.2 6.3 reshape.236
  26.5 15.0 %fusion.13 = bf16[3072,512]{0,1:T(8,128)(2,1)} fusion(bf16[3072,512]{0,1:T(8,128)(2,1)S(1)} %reshape.236, bf16[3072,3072]{1,0:T(8,128)(2,1)} %bitcast.115), kind=kOutput, calls=%fused_computation.28 | convolution fusion | flops 9665249280 | bytes 25165824 | tf_op jit(solution)/shard_map/dot_general | solution.py:76
  41.5 7.3 reshape.238
  48.7 4.9 copy.55
  53.6 7.3 all-to-all-start
  61.3 5.4 copy.53
  66.7 9.8 copy.58
  76.7 0.6 add_multiply_fusion.1
  77.5 8.6 fusion.28
  86.1 46.2 %all-to-all-done = bf16[1,2,1536,256,2]{2,4,1,0,3:T(2,128)(2,1)S(1)} async-done(((bf16[1,2,1536,256,2]{2,4,1,0,3:T(2,128)(2,1)}), bf16[1,2,1536,256,2]{2,4,1,0,3:T(2,128)(2,1)S(1)}, u32[]{:S(2)}, u32[]{:S(2)}) %all-to-all-start) | async-done | bytes 3145760 | tf_op jit(solution)/shard_map/all_to_all | solution.py:80
  132.3 1.6 copy-done.2
  133.9 15.9 %convert_bitcast_fusion = bf16[1,1024,8,2,2,32]{1,5,4,3,2,0:T(8,128)(2,1)} fusion(bf16[8,1536,1024]{2,1,0:T(8,128)(2,1)} %param.11, bf16[1,2,1536,32,8,2]{2,5,1,4,3,0:T(2,128)(2,1)} %bitcast.109), kind=kOutput, calls=%fused_computation.40 | convolution fusion | flops 3222274048 | bytes 30408704 | tf_op jit(solution)/shard_map/obtl,rfbtok->blofkr/dot_general | solution.py:86
  149.8 5.8 fusion.12
  155.9 1289.7 %while.30 = (s32[]{:T(128)}, f32[1024,8,4]{1,2,0:T(4,128)S(1)}, f32[4,1024,8,4,8]{1,4,3,2,0:T(8,128)}, f32[4,1024,8,4,8]{1,4,0,3,2:T(8,128)}, f32[4]{0:T(128)S(1)}, /*index=5*/f32[4,1024,8,8]{3,2,1,0:T(8,128)}, s32[]{:T(128)}) while((s32[]{:T(128)}, f32[1024,8,4]{1,2,0:T(4,128)S(1)}, f32[4,1024,8,4,8]{1,4,3,2,0:T(8,128)}, ...), condition=%wide.region_2.3_spmd.clone, body=%wide.region_1.2_spmd.clone.sunk | while | flops 25722896 | bytes 31065248 | solution.py:59
  156.2 1.3 constant_dynamic-slice_fusion.5
  157.5 13.4 copy.96
  171.4 0.7 broadcast_multiply_fusion.6
  172.1 298.3 %fusion.34 = f32[1024,8,4,8]{1,3,2,0:T(8,128)} fusion(f32[1,1024,8,4,8]{4,2,3,1,0:T(8,128)} %copy.96, f32[8]{0:T(128)S(1)} %compare_convert_fusion.2, f32[1024,8,4]{1,2,0:T(4,128)S(1)} %bitcast.104, f32[4,1024,8,8]{3,2,1,0:T(8,128)} %get-tuple-element.355, s32[]{:T(128)} %get-tuple-element.343), kind=kOutput, calls=%fused_computation.10.clone.1 | convolution fusion | flops 25690112 | bytes 22151712 | tf_op jit(solution)/shard_map/while/body/eval_jaxpr/lij,locj->loci/dot_general | solution.py:49
  470.4 9.9 copy.97
  480.3 1.0 constant_dynamic-update-slice_fusion.2
  481.4 7.9 slice.55
  489.5 1.3 constant_dynamic-slice_fusion.5
  490.8 13.4 copy.96
  504.8 0.7 broadcast_multiply_fusion.6
  505.5 283.0 %fusion.34 = f32[1024,8,4,8]{1,3,2,0:T(8,128)} fusion(f32[1,1024,8,4,8]{4,2,3,1,0:T(8,128)} %copy.96, f32[8]{0:T(128)S(1)} %compare_convert_fusion.2, f32[1024,8,4]{1,2,0:T(4,128)S(1)} %bitcast.104, f32[4,1024,8,8]{3,2,1,0:T(8,128)} %get-tuple-element.355, s32[]{:T(128)} %get-tuple-element.343), kind=kOutput, calls=%fused_computation.10.clone.1 | convolution fusion | flops 25690112 | bytes 22151712 | tf_op jit(solution)/shard_map/while/body/eval_jaxpr/lij,locj->loci/dot_general | solution.py:49
  788.5 9.9 copy.97
  798.4 1.0 constant_dynamic-update-slice_fusion.2
  799.4 7.9 slice.55
  807.6 1.3 constant_dynamic-slice_fusion.5
  808.9 13.4 copy.96
  822.9 0.7 broadcast_multiply_fusion.6
  823.6 283.0 %fusion.34 = f32[1024,8,4,8]{1,3,2,0:T(8,128)} fusion(f32[1,1024,8,4,8]{4,2,3,1,0:T(8,128)} %copy.96, f32[8]{0:T(128)S(1)} %compare_convert_fusion.2, f32[1024,8,4]{1,2,0:T(4,128)S(1)} %bitcast.104, f32[4,1024,8,8]{3,2,1,0:T(8,128)} %get-tuple-element.355, s32[]{:T(128)} %get-tuple-element.343), kind=kOutput, calls=%fused_computation.10.clone.1 | convolution fusion | flops 25690112 | bytes 22151712 | tf_op jit(solution)/shard_map/while/body/eval_jaxpr/lij,locj->loci/dot_general | solution.py:49
  1106.6 9.9 copy.97
  1116.5 1.0 constant_dynamic-update-slice_fusion.2
  1117.5 7.9 slice.55
  1125.7 1.3 constant_dynamic-slice_fusion.5
  1127.0 13.4 copy.96
  1140.9 0.7 broadcast_multiply_fusion.6
  1141.6 283.0 %fusion.34 = f32[1024,8,4,8]{1,3,2,0:T(8,128)} fusion(f32[1,1024,8,4,8]{4,2,3,1,0:T(8,128)} %copy.96, f32[8]{0:T(128)S(1)} %compare_convert_fusion.2, f32[1024,8,4]{1,2,0:T(4,128)S(1)} %bitcast.104, f32[4,1024,8,8]{3,2,1,0:T(8,128)} %get-tuple-element.355, s32[]{:T(128)} %get-tuple-element.343), kind=kOutput, calls=%fused_computation.10.clone.1 | convolution fusion | flops 25690112 | bytes 22151712 | tf_op jit(solution)/shard_map/while/body/eval_jaxpr/lij,locj->loci/dot_general | solution.py:49
  1424.6 9.9 copy.97
  1434.6 1.0 constant_dynamic-update-slice_fusion.2
  1435.6 7.9 slice.55
  1445.6 2.5 broadcast.251.clone2
  1448.1 25.1 %while.29 = (s32[]{:T(128)}, f32[1024,8,4]{0,2,1:T(4,128)S(1)}, f32[4,1024,8,4,8]{1,4,0,3,2:T(8,128)}, f32[4,1024,8,4,8]{1,4,3,2,0:T(8,128)}, f32[4]{0:T(128)S(1...) while((s32[]{:T(128)}, f32[1024,8,4]{0,2,1:T(4,128)S(1)}, f32[4,1024,8,4,8]{1,4,0,3,2:T(8,128)}, ...), condition=%wide.region_4.5_spmd, body=%wide.region_3.4_spmd.sunk | while | flops 622595 | bytes 6402173 | solution.py:60
  1448.1 1.0 constant_dynamic-slice_fusion.4
  1449.2 0.6 dynamic_slice.65
  1449.8 0.6 broadcast_multiply_fusion.5
  1450.4 2.4 bitcast_dynamic-update-slice_fusion.2
  1452.8 1.3 dynamic-slice_bitcast_fusion.2
  1454.4 1.0 constant_dynamic-slice_fusion.4
  1455.5 0.6 dynamic_slice.65
  1456.7 2.4 bitcast_dynamic-update-slice_fusion.2
  1459.1 1.3 dynamic-slice_bitcast_fusion.2
  1460.6 1.0 constant_dynamic-slice_fusion.4
  1461.8 0.6 dynamic_slice.65
  1462.9 2.5 bitcast_dynamic-update-slice_fusion.2
  1465.4 1.3 dynamic-slice_bitcast_fusion.2
  1466.9 1.0 constant_dynamic-slice_fusion.4
  1468.1 0.6 dynamic_slice.65
  1469.3 2.4 bitcast_dynamic-update-slice_fusion.2
  1471.7 1.3 dynamic-slice_bitcast_fusion.2
  1473.2 5.4 copy.65
  (58 shorter events, 6.6 us)
Async XLA Ops:
  53.6 7.6 copy-start.3
  53.6 78.7 %all-to-all-start = ((bf16[1,2,1536,256,2]{2,4,1,0,3:T(2,128)(2,1)}), bf16[1,2,1536,256,2]{2,4,1,0,3:T(2,128)(2,1)S(1)}, u32[]{:S(2)}, u32[]{:S(2)}) async-start(bf16[1,2,1536,256,2]{2,4,1,0,3:T(2,128)(2,1)} %copy.55), calls=%async_computation | async-start | bytes 6291456 | tf_op jit(solution)/shard_map/all_to_all | solution.py:80
  66.7 9.8 copy-start.4
  132.3 1.6 copy-start.2
  133.9 15.9 %copy-start = (f32[1024,8,128]{0,2,1:T(8,128)S(1)}, f32[1024,8,128]{0,2,1:T(8,128)}, u32[]{:S(2)}) copy-start(f32[1024,8,128]{0,2,1:T(8,128)} %copy.53) | copy-start | bytes 12582916
  133.9 15.9 %copy-start.1 = (f32[1024,8,4,31]{0,3,2,1:T(8,128)S(1)}, f32[1024,8,4,31]{0,3,2,1:T(8,128)}, u32[]{:S(2)}) copy-start(f32[1024,8,4,31]{0,3,2,1:T(8,128)} %get-tuple-element.258) | copy-start | bytes 12189700
  1445.6 2.5 copy-start.5
where the time goes:
time: 1490 us; the launch traced here: 1480 us
  matrix products  1180 us (79%)
  local copies, waits for them, and re-layouts  207 us (14%)
  waiting for transfers between devices  46.2 us (3%)
  other arithmetic  36.5 us (2%)
    dot_general x4, matrix products, forward(): jnp.einsum('lij,locj->loci', matrix, block, precision=lax.Precision.HIGHEST)  1150 us
    dynamic_slice x24, local copies, waits for them, and re-layouts, radial_step(): lax.scan(forward, start_carry, (block_inverse, blocks, lower_link))  67.8 us
    all_to_all x1, waiting for transfers between devices, body(): lax.all_to_all(fourier_modes, 'rad', split_axis=3, concat_axis=0, tiled=T...  46.2 us
    dynamic_update_slice x8, local copies, waits for them, and re-layouts, radial_step(): lax.scan(forward, start_carry, (block_inverse, blocks, lower_link))  43.8 us
    slice x4, local copies, waits for them, and re-layouts, forward(): return (result[..., blk_size - 1], result)  31.7 us
  transfers between devices with their start and end apart: 1, of which 1 were waited for; matrix products, arithmetic and copies ran while one was open for 2% of the time, Pallas kernels for 0%

commit v1 on v0

v1 whole, which is shorter than its diff:
```python
import functools
import math

import jax
import jax.numpy as jnp
import numpy as np
from jax import lax
from jax.experimental import pallas as pl
from jax.experimental.pallas import tpu as pltpu
from jax.sharding import PartitionSpec as P

LANES = 128


def trig_factors(orders, quarter, lon_count):
    step = 2.0 * math.pi / lon_count
    coarse_count = lon_count // LANES
    coarse = (orders[:, None] * jnp.arange(coarse_count, dtype=jnp.int32)) % coarse_count * LANES
    fine = orders[:, None] * jnp.arange(LANES, dtype=jnp.int32) + quarter[:, None] * (lon_count // 4)
    coarse_angle = coarse.astype(jnp.float32) * step
    fine_angle = (fine % lon_count).astype(jnp.float32) * step
    scale = 1.0 / math.sqrt(lon_count)
    return (
        jnp.cos(coarse_angle),
        jnp.sin(coarse_angle),
        jnp.cos(fine_angle) * scale,
        jnp.sin(fine_angle) * scale,
    )


def fourier_kernel(ca, sa, cb, sb, x, out, table):
    @pl.when(pl.program_id(0) == 0)
    def _():
        for a in range(ca.shape[1]):
            value = ca[:, a : a + 1] * cb[...] - sa[:, a : a + 1] * sb[...]
            table[:, a * LANES : (a + 1) * LANES] = value.astype(jnp.bfloat16)

    out[...] = lax.dot_general(
        table[...], x[...], (((1,), (1,)), ((), ())), preferred_element_type=jnp.float32
    ).astype(jnp.bfloat16)


def fourier(factors, rows):
    modes = factors[0].shape[0]
    count, lon_count = rows.shape
    tile = 512 if count % 512 == 0 else count
    whole = lambda v: pl.BlockSpec(v.shape, lambda i: (0, 0))
    return pl.pallas_call(
        fourier_kernel,
        grid=(count // tile,),
        in_specs=[whole(v) for v in factors] + [pl.BlockSpec((tile, lon_count), lambda i: (i, 0))],
        out_specs=pl.BlockSpec((modes, tile), lambda i: (0, i)),
        out_shape=jax.ShapeDtypeStruct((modes, count), jnp.bfloat16),
        scratch_shapes=[pltpu.VMEM((modes, lon_count), jnp.bfloat16)],
        name="fourier",
    )(*factors, rows)


def coefficient_rows(inverses, shells):
    degrees, blocks, size, _ = inverses.shape
    spacing = 0.65 / (shells + 1)
    radius = 0.35 + 0.65 * (np.arange(shells) + 1.0) / (shells + 1)
    ratios = spacing / radius
    lower = -0.5 * (1.0 - ratios[0::size])
    upper = -0.5 * (1.0 + ratios[size - 1 :: size])
    inv = jnp.transpose(inverses, (1, 2, 3, 0))
    kinds = []
    for d in range(size):
        kinds.append(jnp.stack([inv[:, i, (i + d) % size] for i in range(size)], axis=1))
    low = jnp.asarray(-lower, jnp.float32)[:, None, None]
    up = jnp.asarray(-upper, jnp.float32)[:, None, None]
    zero = jnp.zeros((1, size, degrees), jnp.float32)
    first = low * inv[:, :, 0]
    last = up * inv[:, :, size - 1]
    wide = lambda v: jnp.broadcast_to(v[:, None], (v.shape[0], size, degrees))
    kinds.append(jnp.concatenate([zero, first[1:]]))
    kinds.append(jnp.concatenate([zero, zero, wide(first[1:-1, size - 1])]))
    kinds.append(jnp.concatenate([last[:-1], zero]))
    kinds.append(jnp.concatenate([wide(last[1:-1, 0]), zero, zero]))
    return jnp.stack(kinds).reshape(len(kinds), blocks * size, degrees)


def spread_kernel(rows, out):
    value = rows[0]
    out[0] = jnp.transpose(jnp.concatenate([value] * (LANES // value.shape[0]), axis=0))


def spread(rows):
    kinds, width, degrees = rows.shape
    return pl.pallas_call(
        spread_kernel,
        grid=(kinds,),
        in_specs=[pl.BlockSpec((1, width, degrees), lambda i: (i, 0, 0))],
        out_specs=pl.BlockSpec((1, degrees, LANES), lambda i: (i, 0, 0)),
        out_shape=jax.ShapeDtypeStruct((kinds, degrees, LANES), jnp.float32),
        name="spread",
    )(rows)


def lane_constants(shells):
    spacing = 0.65 / (shells + 1)
    shell = np.arange(LANES) % shells
    radius = 0.35 + 0.65 * (shell + 1.0) / (shells + 1)
    half = 0.5 * spacing / radius
    table = np.zeros((8, LANES), np.float32)
    table[0] = np.where(shell < shells - 1, 0.5 + half, 0.0)
    table[1] = np.where(shell > 0, 0.5 - half, 0.0)
    table[2] = -0.5 * spacing * spacing / (radius * radius)
    return jnp.asarray(table)


def solve_kernel(bounds, modes, pick, legendre, coef, lanes, state, out, arranged, band, *, first, slots, size):
    slot = pl.program_id(0)
    degrees = legendre.shape[2]
    lat = legendre.shape[1]
    half = arranged.shape[1] // 2

    @pl.when(slot == 0)
    def _():
        for f in range(2):
            part = jnp.dot(
                pick[...], modes[:, f * lat : (f + 1) * lat], preferred_element_type=jnp.float32
            ).astype(jnp.bfloat16)
            for s in range(slots):
                arranged[s, f * half : (f + 1) * half, :] = part[s * half : (s + 1) * half]

    product = jnp.dot(arranged[slot], legendre[0], preferred_element_type=jnp.float32)
    band[...] = jnp.transpose(product.astype(jnp.bfloat16)).astype(jnp.float32)

    mine = first + slot
    low = bounds[0, mine]
    high = bounds[1, mine]
    offset = bounds[2, 0]
    tile = min(64, degrees)
    shape = (tile, LANES)
    lane = lax.broadcasted_iota(jnp.int32, shape, 1)
    group = lane - lane % size
    around = [group + (lane + d) % size for d in range(size)]
    before = jnp.maximum(group - 1, 0)
    after = jnp.minimum(group + size, LANES - 1)
    row = lax.broadcasted_iota(jnp.int32, shape, 0)
    take = lambda v, index: jnp.take_along_axis(v, index, axis=1, mode="promise_in_bounds")

    def piece(n, carry):
        start = pl.multiple_of(n * tile, tile)
        here = pl.ds(start, tile)
        spread_rows = pl.ds(start * 8 + mine, tile, stride=8)
        now = state[spread_rows, :]
        degree = row + (start + offset)
        live = (degree >= low) & (degree < high)
        source = jnp.where(live, band[here, :], 0.0)
        term = (degree * (degree + 1)).astype(jnp.float32)
        right = lanes[0:1, :] * pltpu.roll(now, LANES - 1, 1) + lanes[1:2, :] * pltpu.roll(now, 1, 1)
        right = right + (lanes[2:3, :] * term) * now + source
        value = coef[0, here, :] * right
        for d in range(1, size):
            value = value + coef[d, here, :] * take(right, around[d])
        link = take(value, before)
        chain = link
        for _ in range(2):
            chain = link + coef[size + 1, here, :] * pltpu.roll(chain, size, 1)
        value = value + coef[size, here, :] * chain
        link = take(value, after)
        chain = link
        for _ in range(2):
            chain = link + coef[size + 3, here, :] * pltpu.roll(chain, LANES - size, 1)
        out[spread_rows, :] = value + coef[size + 2, here, :] * chain
        return carry

    lax.fori_loop(0, degrees // tile, piece, 0)


def legendre_solve(bounds, modes, legendre, coef, lanes, state, first, slots, size):
    shells = modes.shape[0] // (2 * slots)
    order, lat, degrees = legendre.shape
    wanted = np.arange(2 * slots * shells)
    place = (wanted % shells) * (2 * slots) + wanted // shells
    pick = (jnp.asarray(place, jnp.int32)[:, None] == jnp.arange(wanted.size, dtype=jnp.int32)).astype(jnp.bfloat16)
    vmem = pl.BlockSpec(memory_space=pltpu.VMEM)
    return pl.pallas_call(
        functools.partial(solve_kernel, first=first, slots=slots, size=size),
        grid=(slots,),
        in_specs=[
            pl.BlockSpec(memory_space=pltpu.SMEM),
            vmem,
            vmem,
            pl.BlockSpec((1, lat, degrees), lambda s: (first + s, 0, 0)),
            vmem,
            vmem,
            vmem,
        ],
        out_specs=vmem,
        out_shape=jax.ShapeDtypeStruct(state.shape, jnp.float32),
        scratch_shapes=[
            pltpu.VMEM((slots, 4 * shells, lat), jnp.bfloat16),
            pltpu.VMEM((degrees, LANES), jnp.float32),
        ],
        compiler_params=pltpu.CompilerParams(vmem_limit_bytes=60 * 1024 * 1024),
        name="legendre_solve",
    )(bounds, modes, pick, legendre, coef, lanes, state)


def body(nonlinear_samples, legendre, assign, counts, spectral_state, inverses):
    rad_local, fields, lat_local, lon_count = nonlinear_samples.shape
    order_total = assign.shape[0]
    order_local = legendre.shape[0]
    degree_local = spectral_state.shape[0]
    shells = spectral_state.shape[2] // 4
    size = inverses.shape[2]
    bands = lax.axis_size("lat")
    devices = lax.axis_size("rad")
    lat_total = lat_local * bands

    rows = nonlinear_samples.reshape(rad_local * fields * lat_local, lon_count)
    orders = jnp.repeat(assign, 2)
    quarter = jnp.arange(2 * order_total, dtype=jnp.int32) % 2
    modes = fourier(trig_factors(orders, quarter, lon_count), rows)
    modes = modes.reshape(devices, 2 * order_local, rows.shape[0])
    moved = lax.all_to_all(modes, "rad", split_axis=0, concat_axis=0, tiled=True)
    if bands > 1:
        legendre = lax.all_to_all(legendre, "lat", split_axis=2, concat_axis=1, tiled=True)
        moved = moved.reshape(devices, 2 * order_local, fields, lat_local)
        moved = lax.all_gather(moved, "lat", axis=3, tiled=True)
    moved = moved.reshape(devices * 2 * order_local, fields * lat_total)

    rad_position = lax.axis_index("rad")
    lat_position = lax.axis_index("lat")
    mine = lax.dynamic_slice_in_dim(assign, rad_position * order_local, order_local, 0)
    ids = jnp.arange(order_total, dtype=jnp.int32)
    live = jnp.sum(jnp.where(mine[:, None] == ids[None, :], counts[None, :], 0), axis=1)
    offset = jnp.broadcast_to(lat_position * degree_local, mine.shape).astype(jnp.int32)
    bounds = jnp.stack([mine, mine + live, offset])

    coef = spread(coefficient_rows(inverses, shells))
    state = spectral_state.reshape(degree_local * order_local, 4 * shells)
    out = legendre_solve(bounds, moved, legendre, coef, lane_constants(shells), state, 0, order_local, size)
    return out.reshape(spectral_state.shape)


def solution(mesh):
    return jax.shard_map(
        body,
        mesh=mesh,
        in_specs=(
            P("rad", None, "lat", None),
            P("rad", "lat", None),
            P(),
            P(),
            P("lat", "rad", None),
            P("lat", None, None, None),
        ),
        out_specs=P("lat", "rad", None),
        check_vma=False,
    )
```

time: 1490 us -> 203 us (0.14)
  matrix products: 1180 us -> 0 us
  local copies, waits for them, and re-layouts: 207 us -> 42.8 us
  Pallas kernels: 0 us -> 125 us
  other arithmetic: 36.5 us -> 7 us
  waiting for transfers between devices: 46.2 us -> 19.1 us
    dot_general x6 -> x0, matrix products: 1180 us -> none  [the longest x4 1150 us: forward(): jnp.einsum('lij,locj->loci', matrix, block, precision=lax.Precision.HIGHEST)]
    pallas_call x0 -> x3, Pallas kernels: none -> 125 us  [the longest x1 98.4 us: legendre_solve(): pl.pallas_call(functools.partial(solve_kernel, first=first, slots=slots,...]
    dynamic_slice x24 -> x0, local copies, waits for them, and re-layouts: 67.8 us -> none  [radial_step(): lax.scan(forward, start_carry, (block_inverse, blocks, lower_link))]
    dynamic_update_slice x8 -> x0, local copies, waits for them, and re-layouts: 43.8 us -> none  [radial_step(): lax.scan(forward, start_carry, (block_inverse, blocks, lower_link))]
    slice x11 -> x4, local copies, waits for them, and re-layouts: 40.5 us -> 2.59 us  [the longest x1 1.86 us: coefficient_rows(): last = up * inv[:, :, size - 1]]
    all_to_all x1, waiting for transfers between devices: 46.2 us -> 19.1 us  [body(): lax.all_to_all(modes, 'rad', split_axis=0, concat_axis=0, tiled=True)]
    reshape x4 -> x0, local copies, waits for them, and re-layouts: 23.8 us -> none  [the longest x2 12.1 us: body(): fourier_modes.reshape(rad_local, 2, lat_local, order_total, 2)]
    another operation x2 -> x17, local copies, waits for them, and re-layouts: 8.26 us -> 23.9 us  [the longest x12 21.9 us: coefficient_rows(): jnp.stack([inv[:, i, (i + d) % size] for i in range(size)], axis=1)]
  transfers between devices with their start and end apart: 1 -> 1, of which waited for: 1 -> 1; matrix products, arithmetic and copies ran while one was open for 2% -> 21% of each run, Pallas kernels for 0% -> 4%
where the time goes in v1:
time: 203 us; the launch traced here: 202 us
  Pallas kernels  125 us (62%)
  local copies, waits for them, and re-layouts  42.8 us (21%)
  waiting for transfers between devices  19.1 us (9%)
  starting transfers between devices  7.51 us (4%)
  other arithmetic  7 us (3%)
    pallas_call x1, Pallas kernels, legendre_solve(): pl.pallas_call(functools.partial(solve_kernel, first=first, slots=slots,...  98.4 us
    another operation x12, local copies, waits for them, and re-layouts, coefficient_rows(): jnp.stack([inv[:, i, (i + d) % size] for i in range(size)], axis=1)  21.9 us
    all_to_all x1, waiting for transfers between devices, body(): lax.all_to_all(modes, 'rad', split_axis=0, concat_axis=0, tiled=True)  19.1 us
    pallas_call x1, Pallas kernels, fourier(): pl.pallas_call(fourier_kernel, grid=(count // tile,), in_specs=[whole(v)...  17.9 us
    unnamed x45, local copies, waits for them, and re-layouts  14.1 us
    pallas_call x1, Pallas kernels, spread(): pl.pallas_call(spread_kernel, grid=(kinds,), in_specs=[pl.BlockSpec((1, w...  9.06 us
    all_to_all x1, starting transfers between devices, body(): lax.all_to_all(modes, 'rad', split_axis=0, concat_axis=0, tiled=True)  7.51 us
  transfers between devices with their start and end apart: 1, of which 1 were waited for; matrix products, arithmetic and copies ran while one was open for 21% of the time, Pallas kernels for 4%

profile of v1, /device:TPU:0, one launch (start us, length us, event | category | flops | bytes accessed | tf_op | source)
XLA Modules:
  0.0 201.9 jit_solution(5195297100564111225)
XLA Ops:
  0.0 0.8 broadcast_in_dim.24
  0.8 0.1 mul.97
  0.9 2.0 fusion.10
  2.9 2.2 %sine_multiply_fusion = (f32[512,128]{1,0:T(8,128)}, f32[512,128]{1,0:T(8,128)}) fusion(s32[512]{0:T(512)S(1)} %fusion.16, s32[512]{0:T(512)S(1)} %mul.97), kind=kLoop, calls=%fused_computation.9 | loop fusion | flops 786432 | bytes 528384 | tf_op jit(solution)/shard_map/mul | solution.py:27
  5.1 17.9 %fourier.1 = bf16[512,3072]{1,0:T(8,128)(2,1)} custom-call(f32[512,24]{1,0:T(8,128)} %get-tuple-element.74.ca, f32[512,24]{1,0:T(8,128)} %get-tuple-element.73.sa, f32[512,128]{1,0:T(8,128)} %get-tuple-element.72.cb, f32[512,128]{1,0:T(8,128)} %get-tuple-element.71.sb, bf16[3072,3072]{1,0:T(8,128)(2,1)} %bitcast.290), custom_call_target="tpu_custom_call" | custom-call | tf_op jit(solution)/shard_map/fourier/pallas_call | solution.py:48
  23.0 0.0 copy-start.5
  23.0 7.5 %all-to-all-start = ((bf16[32,16,3072]{2,1,0:T(8,128)(2,1)}), bf16[32,16,3072]{2,1,0:T(8,128)(2,1)S(1)}, u32[]{:S(2)}, u32[]{:S(2)}) async-start(bf16[32,16,3072]{2,1,0:T(8,128)(2,1)} %bitcast.292), calls=%async_computation | async-start | bytes 6291456 | tf_op jit(solution)/shard_map/all_to_all | solution.py:219
  30.5 1.9 fusion.20
  32.4 0.0 copy-done.11
  32.4 0.1 bitcast_multiply_fusion.1
  32.5 0.6 slice.343
  33.2 0.0 copy-done.15
  33.2 0.1 broadcast.79
  33.2 0.7 reshape.101
  33.9 0.0 copy-done.13
  33.9 0.1 slice.346
  34.0 0.0 copy-done.5
  34.0 0.6 dynamic_slice.3
  34.5 0.6 pad.6.clone
  35.1 0.1 mul.116
  35.2 0.6 mul.117
  35.8 0.6 copy.304
  36.4 0.1 slice_multiply_fusion
  36.5 0.6 copy.303
  37.1 2.8 %slice_bitcast_fusion = (f32[4,1,1024]{2,1,0:T(1,128)}, f32[4,1,1024]{2,1,0:T(1,128)}, f32[4,1,1024]{2,1,0:T(1,128)}, f32[4,1,1024]{2,1,0:T(1,128)}, f32[4,1,102...) fusion(f32[4,8,8,1024]{3,2,1,0:T(8,128)} %bitcast.295), kind=kLoop, calls=%fused_computation.37 | loop fusion | bytes 622592 | tf_op jit(solution)/shard_map/stack;squeeze | solution.py:69
  40.0 2.9 %slice_bitcast_fusion.8 = (f32[4,1,1024]{2,1,0:T(1,128)S(1)}, f32[4,1,1024]{2,1,0:T(1,128)}, f32[4,1,1024]{2,1,0:T(1,128)}, f32[4,1,1024]{2,1,0:T(1,128)}, f32[4...) fusion(f32[4,8,8,1024]{3,2,1,0:T(8,128)} %bitcast.296), kind=kLoop, calls=%fused_computation.45 | loop fusion | bytes 622592 | tf_op jit(solution)/shard_map/stack;squeeze | solution.py:69
  42.9 0.2 stack.85
  43.1 2.1 %slice_bitcast_fusion.16 = (f32[4,1,1024]{2,1,0:T(1,128)}, f32[4,1,1024]{2,1,0:T(1,128)}, f32[4,1,1024]{2,1,0:T(1,128)}, f32[4,1,1024]{2,1,0:T(1,128)}, f32[4,1,...) fusion(f32[4,8,8,1024]{3,2,1,0:T(8,128)} %bitcast.297), kind=kLoop, calls=%fused_computation.53 | loop fusion | bytes 229376 | tf_op jit(solution)/shard_map/stack;squeeze | solution.py:69
  45.1 1.0 stack.73
  46.2 1.7 stack.75
  47.8 2.9 %slice_bitcast_fusion.1 = (f32[4,1,1024]{2,1,0:T(1,128)}, f32[4,1,1024]{2,1,0:T(1,128)}, f32[4,1,1024]{2,1,0:T(1,128)}, f32[4,1,1024]{2,1,0:T(1,128)}, f32[4,1,1...) fusion(f32[4,8,8,1024]{3,2,1,0:T(8,128)} %bitcast.298), kind=kLoop, calls=%fused_computation.38 | loop fusion | bytes 622592 | tf_op jit(solution)/shard_map/stack;squeeze | solution.py:69
  50.7 1.7 stack.87
  52.4 1.7 stack.83
  54.0 1.7 stack.77
  55.7 1.7 stack.81
  57.4 1.6 stack.79
  59.0 0.0 copy-start.8
  59.0 0.0 copy-start.10
  59.0 0.0 copy-start.3
  59.1 0.7 bitcast_dynamic-update-slice_fusion.10
  59.7 1.6 bitcast_dynamic-update-slice_fusion.9
  61.3 1.6 bitcast_dynamic-update-slice_fusion.8
  62.9 1.6 bitcast_dynamic-update-slice_fusion.7
  64.4 1.6 bitcast_dynamic-update-slice_fusion.6
  66.0 1.6 bitcast_dynamic-update-slice_fusion.5
  67.6 0.7 bitcast_dynamic-update-slice_fusion.4
  68.2 0.0 copy-done.1
  68.2 0.7 bitcast_dynamic-update-slice_fusion.3
  68.9 0.0 copy-done.2
  68.9 0.7 bitcast_dynamic-update-slice_fusion.2
  69.5 0.7 bitcast_dynamic-update-slice_fusion.1
  70.2 0.7 fusion.15
  71.0 0.7 bitcast_dynamic-update-slice_fusion.rows
  71.6 0.0 copy-start.7
  71.6 9.1 %spread.1.coef = f32[12,1024,128]{2,1,0:T(8,128)} custom-call(f32[12,32,1024]{2,1,0:T(8,128)} %bitcast_dynamic-update-slice_fusion.rows), custom_call_target="tpu_custom_call" | custom-call | tf_op jit(solution)/shard_map/spread/pallas_call | solution.py:90
  80.7 0.1 dynamic-slice_bitcast_fusion
  80.8 0.2 select_reduce_fusion
  81.0 0.1 add_bitcast_fusion
  81.0 0.7 add_add_fusion.bounds
  81.7 0.0 copy-done.7
  81.7 1.0 fusion.pick
  82.7 19.1 %all-to-all-done = bf16[32,16,3072]{2,1,0:T(8,128)(2,1)S(1)} async-done(((bf16[32,16,3072]{2,1,0:T(8,128)(2,1)}), bf16[32,16,3072]{2,1,0:T(8,128)(2,1)S(1)}, u32[]{:S(2)}, u32[]{:S(2)}) %all-to-all-start) | async-done | bytes 3145760 | tf_op jit(solution)/shard_map/all_to_all | solution.py:219
  101.8 1.7 copy-done
  103.5 98.4 %legendre_solve.1 = f32[8192,128]{1,0:T(8,128)} custom-call(s32[3,8]{1,0:T(4,128)} %add_add_fusion.bounds, bf16[512,3072]{1,0:T(8,128)(2,1)} %bitcast.291, bf16[512,512]{1,0:T(8,128)(2,1)} %fusion.pick, bf16[8,1536,1024]{2,1,0:T(8,128)(2,1)} %legendre.1, f32[12,1024,128]{2,1,0:T(8,128)} %spread.1.coef, f32[8,128]{1,0:T(8,128)} %constant.75.clone.lanes, ...), custom_call_target="tpu_custom_call" | custom-call | tf_op jit(solution)/shard_map/legendre_solve/pallas_call | solution.py:180
  (24 shorter events, 0.1 us)
Async XLA Ops:
  23.0 9.4 %copy-start.11 = (f32[4]{0:T(128)S(1)}, f32[4]{0:T(128)}, u32[]{:S(2)}) copy-start(f32[4]{0:T(128)} %constant.73.clone) | copy-start | bytes 52
  23.0 10.2 %copy-start.15 = (pred[4]{0:T(512)(128)(4,1)S(1)}, pred[4]{0:T(512)(128)(4,1)}, u32[]{:S(2)}) copy-start(pred[4]{0:T(512)(128)(4,1)} %constant.72.clone.1) | copy-start | bytes 16
  23.0 10.9 %copy-start.13 = (f32[4]{0:T(128)S(1)}, f32[4]{0:T(128)}, u32[]{:S(2)}) copy-start(f32[4]{0:T(128)} %constant.74.clone) | copy-start | bytes 52
  23.0 11.0 %copy-start.5 = (s32[256]{0:T(256)S(1)}, s32[256]{0:T(256)}, u32[]{:S(2)}) copy-start(s32[256]{0:T(256)} %param.12) | copy-start | bytes 3076
  23.0 78.8 %all-to-all-start = ((bf16[32,16,3072]{2,1,0:T(8,128)(2,1)}), bf16[32,16,3072]{2,1,0:T(8,128)(2,1)S(1)}, u32[]{:S(2)}, u32[]{:S(2)}) async-start(bf16[32,16,3072]{2,1,0:T(8,128)(2,1)} %bitcast.292), calls=%async_computation | async-start | bytes 6291456 | tf_op jit(solution)/shard_map/all_to_all | solution.py:219
  59.0 9.2 %copy-start.1 = (f32[4,8,1024]{2,1,0:T(8,128)S(1)}, f32[4,8,1024]{2,1,0:T(8,128)}, u32[]{:S(2)}) copy-start(f32[4,8,1024]{2,1,0:T(8,128)} %stack.87) | copy-start | bytes 393220
  59.0 9.9 %copy-start.2 = (f32[3,8,1024]{2,1,0:T(8,128)S(1)}, f32[3,8,1024]{2,1,0:T(8,128)}, u32[]{:S(2)}) copy-start(f32[3,8,1024]{2,1,0:T(8,128)} %slice.343) | copy-start | bytes 294916
  59.0 10.5 %copy-start.4 = (f32[2,1,1024]{2,0,1:T(2,128)S(1)}, f32[2,1,1024]{2,0,1:T(2,128)}, u32[]{:S(2)}) copy-start(f32[2,1,1024]{2,0,1:T(2,128)} %copy.304) | copy-start | bytes 24580
  59.0 11.2 %copy-start.8 = (f32[32]{0:T(128)S(1)}, f32[32]{0:T(128)}, u32[]{:S(2)}) copy-start(f32[32]{0:T(128)} %mul.117) | copy-start | bytes 388
  59.0 11.2 %copy-start.10 = (pred[32]{0:T(512)(128)(4,1)S(1)}, pred[32]{0:T(512)(128)(4,1)}, u32[]{:S(2)}) copy-start(pred[32]{0:T(512)(128)(4,1)} %reshape.101) | copy-start | bytes 100
  59.0 11.9 %copy-start.3 = (f32[2,1,1024]{2,0,1:T(2,128)S(1)}, f32[2,1,1024]{2,0,1:T(2,128)}, u32[]{:S(2)}) copy-start(f32[2,1,1024]{2,0,1:T(2,128)} %copy.303) | copy-start | bytes 24580
  71.6 9.1 %copy-start.6 = (s32[256]{0:T(256)S(1)}, s32[256]{0:T(256)}, u32[]{:S(2)}) copy-start(s32[256]{0:T(256)} %param.12) | copy-start | bytes 3076
  71.6 9.2 %copy-start.9 = (s32[256]{0:T(256)S(1)}, s32[256]{0:T(256)}, u32[]{:S(2)}) copy-start(s32[256]{0:T(256)} %param.13) | copy-start | bytes 3076
  71.6 9.2 %copy-start.14 = (s32[8]{0:T(128)S(1)}, s32[8]{0:T(128)}, u32[]{:S(2)}) copy-start(s32[8]{0:T(128)} %dynamic_slice.3) | copy-start | bytes 100
  71.6 9.4 %copy-start.12 = (s32[3]{0:T(128)S(1)}, s32[3]{0:T(128)}, u32[]{:S(2)}) copy-start(s32[3]{0:T(128)} %pad.6.clone) | copy-start | bytes 40
  71.6 10.1 %copy-start.7 = (s32[512]{0:T(512)S(1)}, s32[512]{0:T(512)}, u32[]{:S(2)}) copy-start(s32[512]{0:T(512)} %constant.76.clone) | copy-start | bytes 6148
  101.8 1.7 copy-start

commit v2 on v1

v2 whole, which is shorter than its diff:
```python
import functools
import math

import jax
import jax.numpy as jnp
import numpy as np
from jax import lax
from jax.experimental import pallas as pl
from jax.experimental.pallas import tpu as pltpu
from jax.sharding import PartitionSpec as P

LANES = 128


def trig_factors(orders, quarter, lon_count):
    step = 2.0 * math.pi / lon_count
    coarse_count = lon_count // LANES
    coarse = (orders[:, None] * jnp.arange(coarse_count, dtype=jnp.int32)) % coarse_count * LANES
    fine = orders[:, None] * jnp.arange(LANES, dtype=jnp.int32) + quarter[:, None] * (lon_count // 4)
    coarse_angle = coarse.astype(jnp.float32) * step
    fine_angle = (fine % lon_count).astype(jnp.float32) * step
    scale = 1.0 / math.sqrt(lon_count)
    return (
        jnp.cos(coarse_angle),
        jnp.sin(coarse_angle),
        jnp.cos(fine_angle) * scale,
        jnp.sin(fine_angle) * scale,
    )


def fourier_kernel(ca, sa, cb, sb, x, out, table):
    @pl.when(pl.program_id(0) == 0)
    def _():
        for a in range(ca.shape[1]):
            value = ca[:, a : a + 1] * cb[...] - sa[:, a : a + 1] * sb[...]
            table[:, a * LANES : (a + 1) * LANES] = value.astype(jnp.bfloat16)

    out[...] = lax.dot_general(
        table[...], x[...], (((1,), (1,)), ((), ())), preferred_element_type=jnp.float32
    ).astype(jnp.bfloat16)


def fourier(factors, rows):
    modes = factors[0].shape[0]
    count, lon_count = rows.shape
    tile = 512 if count % 512 == 0 else count
    whole = lambda v: pl.BlockSpec(v.shape, lambda i: (0, 0))
    return pl.pallas_call(
        fourier_kernel,
        grid=(count // tile,),
        in_specs=[whole(v) for v in factors] + [pl.BlockSpec((tile, lon_count), lambda i: (i, 0))],
        out_specs=pl.BlockSpec((modes, tile), lambda i: (0, i)),
        out_shape=jax.ShapeDtypeStruct((modes, count), jnp.bfloat16),
        scratch_shapes=[pltpu.VMEM((modes, lon_count), jnp.bfloat16)],
        name="fourier",
    )(*factors, rows)


def lane_constants(shells):
    spacing = 0.65 / (shells + 1)
    shell = np.arange(LANES) % shells
    radius = 0.35 + 0.65 * (shell + 1.0) / (shells + 1)
    half = 0.5 * spacing / radius
    table = np.zeros((8, LANES), np.float32)
    table[0] = np.where(shell < shells - 1, 0.5 + half, 0.0)
    table[1] = np.where(shell > 0, 0.5 - half, 0.0)
    table[2] = -0.5 * spacing * spacing / (radius * radius)
    return jnp.asarray(table)


def explicit_kernel(offset, lanes, state, out, *, slots):
    tile = out.shape[2]
    start = offset[0] + pl.program_id(0) * tile
    degree = lax.broadcasted_iota(jnp.int32, (tile, LANES), 0) + start
    term = (degree * (degree + 1)).astype(jnp.float32) * lanes[2:3, :]
    for s in range(slots):
        now = state[pl.ds(s, tile, stride=slots), :]
        right = lanes[0:1, :] * pltpu.roll(now, LANES - 1, 1) + lanes[1:2, :] * pltpu.roll(now, 1, 1)
        out[s] = jnp.transpose(right + term * now)


def explicit_part(offset, lanes, state, slots):
    degrees = state.shape[0] // slots
    tile = min(LANES, degrees)
    return pl.pallas_call(
        functools.partial(explicit_kernel, slots=slots),
        grid=(degrees // tile,),
        in_specs=[
            pl.BlockSpec(memory_space=pltpu.SMEM),
            pl.BlockSpec(lanes.shape, lambda i: (0, 0)),
            pl.BlockSpec((tile * slots, LANES), lambda i: (i, 0)),
        ],
        out_specs=pl.BlockSpec((slots, LANES, tile), lambda i: (0, 0, i)),
        out_shape=jax.ShapeDtypeStruct((slots, LANES, degrees), jnp.float32),
        name="explicit_part",
    )(offset, lanes, state)


def solve_kernel(bounds, modes, pick, legendre, inv, explicit, *rest, first, slots, size, links, aliased):
    if aliased:
        rest = rest[1:]
    out, arranged, right = rest
    slot = pl.program_id(0)
    lat, degrees = legendre.shape[1:]
    half = arranged.shape[1] // 2
    blocks = len(links[0])
    comps = LANES // (blocks * size)

    @pl.when(slot == 0)
    def _():
        for f in range(2):
            part = jnp.dot(
                pick[...], modes[:, f * lat : (f + 1) * lat], preferred_element_type=jnp.float32
            ).astype(jnp.bfloat16)
            for s in range(slots):
                arranged[s, f * half : (f + 1) * half, :] = part[s * half : (s + 1) * half]

    mine = first + slot
    low = bounds[0, mine]
    high = bounds[1, mine]
    offset = bounds[2, 0]
    product = jnp.dot(arranged[slot], legendre[0], preferred_element_type=jnp.float32)
    degree = lax.broadcasted_iota(jnp.int32, product.shape, 1) + offset
    live = (degree >= low) & (degree < high)
    source = product.astype(jnp.bfloat16).astype(jnp.float32)
    right[...] = explicit[0] + jnp.where(live, source, 0.0)

    tile = min(LANES, degrees)
    total = out.shape[0] // degrees

    def piece(n, carry):
        start = pl.multiple_of(n * tile, tile)
        here = pl.ds(start, tile)
        solved = [[None] * blocks for _ in range(comps)]
        for k in range(blocks):
            matrix = [inv[(k * size + j) * size : (k * size + j + 1) * size, here] for j in range(size)]
            for c in range(comps):
                base = (c * blocks + k) * size
                lead = right[base : base + 1, here]
                if k:
                    lead = lead - links[0][k] * solved[c][k - 1][size - 1 : size]
                value = matrix[0] * lead
                for j in range(1, size):
                    value = value + matrix[j] * right[base + j : base + j + 1, here]
                solved[c][k] = value
        for k in range(blocks - 2, -1, -1):
            last = inv[(k + 1) * size * size - size : (k + 1) * size * size, here]
            for c in range(comps):
                solved[c][k] = solved[c][k] - links[1][k] * solved[c][k + 1][0:1] * last
        whole = jnp.concatenate([solved[c][k] for c in range(comps) for k in range(blocks)], axis=0)
        out[pl.ds(start * total + mine, tile, stride=total), :] = jnp.transpose(whole)
        return carry

    lax.fori_loop(0, degrees // tile, piece, 0)


def legendre_solve(bounds, modes, legendre, inv, explicit, previous, first, slots, size):
    shells = modes.shape[0] // (2 * slots)
    order, lat, degrees = legendre.shape
    spacing = 0.65 / (shells + 1)
    radius = 0.35 + 0.65 * (np.arange(shells) + 1.0) / (shells + 1)
    ratios = spacing / radius
    lower = [float(v) for v in -0.5 * (1.0 - ratios[0::size])]
    upper = [float(v) for v in -0.5 * (1.0 + ratios[size - 1 :: size])]
    wanted = np.arange(2 * slots * shells)
    place = (wanted % shells) * (2 * slots) + wanted // shells
    pick = (jnp.asarray(place, jnp.int32)[:, None] == jnp.arange(wanted.size, dtype=jnp.int32)).astype(jnp.bfloat16)
    vmem = pl.BlockSpec(memory_space=pltpu.VMEM)
    in_specs = [
        pl.BlockSpec(memory_space=pltpu.SMEM),
        vmem,
        vmem,
        pl.BlockSpec((1, lat, degrees), lambda s: (first + s, 0, 0)),
        vmem,
        pl.BlockSpec((1, LANES, degrees), lambda s: (first + s, 0, 0)),
    ]
    args = [bounds, modes, pick, legendre, inv, explicit]
    if previous is not None:
        in_specs.append(vmem)
        args.append(previous)
    return pl.pallas_call(
        functools.partial(
            solve_kernel, first=first, slots=slots, size=size, links=(lower, upper), aliased=previous is not None
        ),
        grid=(slots,),
        in_specs=in_specs,
        out_specs=vmem,
        out_shape=jax.ShapeDtypeStruct((degrees * order, LANES), jnp.float32),
        scratch_shapes=[
            pltpu.VMEM((slots, 4 * shells, lat), jnp.bfloat16),
            pltpu.VMEM((LANES, degrees), jnp.float32),
        ],
        input_output_aliases={6: 0} if previous is not None else {},
        compiler_params=pltpu.CompilerParams(vmem_limit_bytes=60 * 1024 * 1024),
        name="legendre_solve",
    )(*args)


def body(nonlinear_samples, legendre, assign, counts, spectral_state, inverses):
    rad_local, fields, lat_local, lon_count = nonlinear_samples.shape
    order_total = assign.shape[0]
    order_local = legendre.shape[0]
    degree_local = spectral_state.shape[0]
    shells = spectral_state.shape[2] // 4
    size = inverses.shape[2]
    bands = lax.axis_size("lat")
    devices = lax.axis_size("rad")
    lat_total = lat_local * bands

    rows = nonlinear_samples.reshape(rad_local * fields * lat_local, lon_count)
    orders = jnp.repeat(assign, 2)
    quarter = jnp.arange(2 * order_total, dtype=jnp.int32) % 2
    modes = fourier(trig_factors(orders, quarter, lon_count), rows)
    modes = modes.reshape(devices, 2 * order_local, rows.shape[0])
    moved = lax.all_to_all(modes, "rad", split_axis=0, concat_axis=0, tiled=True)
    if bands > 1:
        legendre = lax.all_to_all(legendre, "lat", split_axis=2, concat_axis=1, tiled=True)
        moved = moved.reshape(devices, 2 * order_local, fields, lat_local)
        moved = lax.all_gather(moved, "lat", axis=3, tiled=True)
    moved = moved.reshape(devices * 2 * order_local, fields * lat_total)

    rad_position = lax.axis_index("rad")
    lat_position = lax.axis_index("lat")
    mine = lax.dynamic_slice_in_dim(assign, rad_position * order_local, order_local, 0)
    ids = jnp.arange(order_total, dtype=jnp.int32)
    live = jnp.sum(jnp.where(mine[:, None] == ids[None, :], counts[None, :], 0), axis=1)
    offset = jnp.broadcast_to(lat_position * degree_local, mine.shape).astype(jnp.int32)
    bounds = jnp.stack([mine, mine + live, offset])

    inv = jnp.transpose(inverses, (1, 3, 2, 0)).reshape(-1, degree_local)
    state = spectral_state.reshape(degree_local * order_local, 4 * shells)
    explicit = explicit_part(offset[:1], lane_constants(shells), state, order_local)
    out = legendre_solve(bounds, moved, legendre, inv, explicit, None, 0, order_local, size)
    return out.reshape(spectral_state.shape)


def solution(mesh):
    return jax.shard_map(
        body,
        mesh=mesh,
        in_specs=(
            P("rad", None, "lat", None),
            P("rad", "lat", None),
            P(),
            P(),
            P("lat", "rad", None),
            P("lat", None, None, None),
        ),
        out_specs=P("lat", "rad", None),
        check_vma=False,
    )
```

time: 203 us -> 127 us (0.63)
  Pallas kernels: 125 us -> 49.4 us
  waiting for transfers between devices: 19.1 us -> 57.7 us
  local copies, waits for them, and re-layouts: 42.8 us -> 5.67 us
    pallas_call x1, Pallas kernels: 98.4 us -> 22.9 us  [legendre_solve(): pl.pallas_call(functools.partial(solve_kernel, first=first, slots=slots,...]
    all_to_all x1, waiting for transfers between devices: 19.1 us -> 57.7 us  [body(): lax.all_to_all(modes, 'rad', split_axis=0, concat_axis=0, tiled=True)]
    another operation x15 -> x0, local copies, waits for them, and re-layouts: 23.3 us -> none  [the longest x12 21.9 us: coefficient_rows(): jnp.stack([inv[:, i, (i + d) % size] for i in range(size)], axis=1)]
    unnamed x45 -> x8, local copies, waits for them, and re-layouts: 14.1 us -> 1.69 us
    transpose x0 -> x1, local copies, waits for them, and re-layouts: none -> 2.84 us  [body(): inv = jnp.transpose(inverses, (1, 3, 2, 0)).reshape(-1, degree_local)]
    slice x4 -> x0, local copies, waits for them, and re-layouts: 2.59 us -> none  [the longest x1 1.86 us: coefficient_rows(): last = up * inv[:, :, size - 1]]
  transfers between devices with their start and end apart: 1 -> 1, of which waited for: 1 -> 1; matrix products, arithmetic and copies ran while one was open for 21% -> 4% of each run, Pallas kernels for 4% -> 7%
where the time goes in v2:
time: 127 us; the launch traced here: 126 us
  waiting for transfers between devices  57.7 us (45%)
  Pallas kernels  49.4 us (39%)
  starting transfers between devices  7.33 us (6%)
  other arithmetic  6.06 us (5%)
  local copies, waits for them, and re-layouts  5.67 us (4%)
    all_to_all x1, waiting for transfers between devices, body(): lax.all_to_all(modes, 'rad', split_axis=0, concat_axis=0, tiled=True)  57.7 us
    pallas_call x1, Pallas kernels, legendre_solve(): pl.pallas_call(functools.partial(solve_kernel, first=first, slots=slots,...  22.9 us
    pallas_call x1, Pallas kernels, fourier(): pl.pallas_call(fourier_kernel, grid=(count // tile,), in_specs=[whole(v)...  17.9 us
    pallas_call x1, Pallas kernels, explicit_part(): pl.pallas_call(functools.partial(explicit_kernel, slots=slots), grid=(deg...  8.65 us
    all_to_all x1, starting transfers between devices, body(): lax.all_to_all(modes, 'rad', split_axis=0, concat_axis=0, tiled=True)  7.33 us
    transpose x1, local copies, waits for them, and re-layouts, body(): inv = jnp.transpose(inverses, (1, 3, 2, 0)).reshape(-1, degree_local)  2.84 us
  transfers between devices with their start and end apart: 1, of which 1 were waited for; matrix products, arithmetic and copies ran while one was open for 4% of the time, Pallas kernels for 7%

profile of v2, /device:TPU:0, one launch (start us, length us, event | category | flops | bytes accessed | tf_op | source)
XLA Modules:
  0.0 126.2 jit_solution(17419656491658539014)
XLA Ops:
  0.0 0.8 broadcast_in_dim.16
  0.8 0.1 mul.68
  0.9 2.0 %fusion.10 = (f32[512,24]{1,0:T(8,128)}, f32[512,24]{1,0:T(8,128)}) fusion(s32[512]{0:T(512)S(1)} %mul.68), kind=kLoop, calls=%fused_computation.17 | loop fusion | flops 122880 | bytes 100352 | tf_op jit(solution)/shard_map/sin | solution.py:25
  2.9 2.2 %sine_multiply_fusion = (f32[512,128]{1,0:T(8,128)}, f32[512,128]{1,0:T(8,128)}) fusion(s32[512]{0:T(512)S(1)} %fusion.14, s32[512]{0:T(512)S(1)} %mul.68), kind=kLoop, calls=%fused_computation.9 | loop fusion | flops 786432 | bytes 528384 | tf_op jit(solution)/shard_map/mul | solution.py:27
  5.1 17.9 %fourier.1 = bf16[512,3072]{1,0:T(8,128)(2,1)} custom-call(f32[512,24]{1,0:T(8,128)} %get-tuple-element.8.ca, f32[512,24]{1,0:T(8,128)} %get-tuple-element.7.sa, f32[512,128]{1,0:T(8,128)} %get-tuple-element.6.cb, f32[512,128]{1,0:T(8,128)} %get-tuple-element.5.sb, bf16[3072,3072]{1,0:T(8,128)(2,1)} %bitcast.12), custom_call_target="tpu_custom_call" | custom-call | tf_op jit(solution)/shard_map/fourier/pallas_call | solution.py:48
  23.0 0.0 copy-start.1
  23.0 7.3 %all-to-all-start = ((bf16[32,16,3072]{2,1,0:T(8,128)(2,1)}), bf16[32,16,3072]{2,1,0:T(8,128)(2,1)S(1)}, u32[]{:S(2)}, u32[]{:S(2)}) async-start(bf16[32,16,3072]{2,1,0:T(8,128)(2,1)} %bitcast.14), calls=%async_computation | async-start | bytes 6291456 | tf_op jit(solution)/shard_map/all_to_all | solution.py:215
  30.3 0.0 copy-done.1
  30.3 0.1 dynamic_slice.3
  30.4 0.1 pad.2.clone
  30.5 2.8 %copy.13 = f32[4,8,8,1024]{3,2,1,0:T(8,128)} copy(f32[4,8,8,1024]{3,1,2,0:T(8,128)} %bitcast.17) | data formatting | bytes 2097152 | tf_op jit(solution)/shard_map/transpose | solution.py:230
  33.3 0.0 copy-start.3
  33.3 0.0 copy-start.2
  33.3 8.6 %explicit_part.1.explicit = f32[8,128,1024]{2,1,0:T(8,128)} custom-call(s32[1]{0:T(128)} %constant.65.clone.1.offset, f32[8,128]{1,0:T(8,128)} %constant.66.clone.lanes, f32[8192,128]{1,0:T(8,128)} %bitcast.16), custom_call_target="tpu_custom_call" | custom-call | tf_op jit(solution)/shard_map/explicit_part/pallas_call | solution.py:85
  42.0 0.1 dynamic-slice_bitcast_fusion
  42.1 0.0 copy-done.3
  42.1 0.2 select_reduce_fusion
  42.2 0.1 add_bitcast_fusion
  42.3 0.6 add_add_fusion.bounds
  42.9 0.0 copy-done.2
  42.9 1.0 fusion.pick
  43.9 57.7 %all-to-all-done = bf16[32,16,3072]{2,1,0:T(8,128)(2,1)S(1)} async-done(((bf16[32,16,3072]{2,1,0:T(8,128)(2,1)}), bf16[32,16,3072]{2,1,0:T(8,128)(2,1)S(1)}, u32[]{:S(2)}, u32[]{:S(2)}) %all-to-all-start) | async-done | bytes 3145760 | tf_op jit(solution)/shard_map/all_to_all | solution.py:215
  101.7 0.0 copy-start
  101.7 1.7 %copy-done = bf16[32,16,3072]{2,1,0:T(8,128)(2,1)} copy-done((bf16[32,16,3072]{2,1,0:T(8,128)(2,1)}, bf16[32,16,3072]{2,1,0:T(8,128)(2,1)S(1)}, u32[]{:S(2)}) %copy-start) | copy-done | bytes 3145752
  103.3 22.9 %legendre_solve.1 = f32[8192,128]{1,0:T(8,128)} custom-call(s32[3,8]{1,0:T(4,128)} %add_add_fusion.bounds, bf16[512,3072]{1,0:T(8,128)(2,1)} %bitcast.13, bf16[512,512]{1,0:T(8,128)(2,1)} %fusion.pick, bf16[8,1536,1024]{2,1,0:T(8,128)(2,1)} %legendre.1, f32[256,1024]{1,0:T(8,128)} %bitcast.15, f32[8,128,1024]{2,1,0:T(8,128)} %explicit_part.1.explicit), custom_call_target="tpu_custom_call" | custom-call | tf_op jit(solution)/shard_map/legendre_solve/pallas_call | solution.py:181
  (1 shorter events, 0.0 us)
Async XLA Ops:
  23.0 7.3 %copy-start.1 = (s32[256]{0:T(256)S(1)}, s32[256]{0:T(256)}, u32[]{:S(2)}) copy-start(s32[256]{0:T(256)} %param.10) | copy-start | bytes 3076
  23.0 78.7 %all-to-all-start = ((bf16[32,16,3072]{2,1,0:T(8,128)(2,1)}), bf16[32,16,3072]{2,1,0:T(8,128)(2,1)S(1)}, u32[]{:S(2)}, u32[]{:S(2)}) async-start(bf16[32,16,3072]{2,1,0:T(8,128)(2,1)} %bitcast.14), calls=%async_computation | async-start | bytes 6291456 | tf_op jit(solution)/shard_map/all_to_all | solution.py:215
  33.3 8.7 %copy-start.3 = (s32[256]{0:T(256)S(1)}, s32[256]{0:T(256)}, u32[]{:S(2)}) copy-start(s32[256]{0:T(256)} %param.11) | copy-start | bytes 3076
  33.3 9.6 %copy-start.2 = (s32[512]{0:T(512)S(1)}, s32[512]{0:T(512)}, u32[]{:S(2)}) copy-start(s32[512]{0:T(512)} %constant.67.clone) | copy-start | bytes 6148
  101.7 1.7 %copy-start = (bf16[32,16,3072]{2,1,0:T(8,128)(2,1)}, bf16[32,16,3072]{2,1,0:T(8,128)(2,1)S(1)}, u32[]{:S(2)}) copy-start(bf16[32,16,3072]{2,1,0:T(8,128)(2,1)S(1)} %all-to-all-done) | copy-start | bytes 9437188
